TPU v7x, 32 devices: a whole 2x2x4 slice. The times are simulated.
32 devices in a mesh: groups: 2 (over x), sample: 16 (over z, y, core).
Axes of the slice: x: 2, y: 2, z: 4, core: 2. Of those that a mesh axis runs over, the one named last changes fastest.
Arguments:
- prompt_states: bfloat16 [16384, 8192], P(('groups', 'sample')), parts along dimension 0, may hold values from -6 to 6
- page_table: int32 [128], P('groups'), parts along dimension 0, may hold values from 0 to 63, each once
- step_states: bfloat16 [2, 64, 8192], P(None, 'groups'), parts along dimension 1, may hold values from -15 to 15
- sample_order: int32 [64], P('groups'), parts along dimension 0, may hold values from 0 to 31, each once
- key_weight: bfloat16 [8192, 512], P('sample'), may hold values from -0.088388348 to 0.088388348
- value_weight: bfloat16 [8192, 512], P('sample'), may hold values from -0.0625 to 0.0625
- query_weight: bfloat16 [8192, 4096], P(None, 'sample'), may hold values from -0.121533978 to 0.121533978
- out_weight: bfloat16 [4096, 8192], P('sample'), may hold values from -0.125 to 0.125
Outputs:
- attn_out: bfloat16 [2, 64, 8192], P(None, 'groups', 'sample'), parts along dimension 1
There are 2 independent parts, one for each index of `groups`. A program takes and returns all parts, laid end to end along the dimension named above; an argument that names none is the same for every part. Nothing has to cross between parts.
Inputs may be any that keep to these rules, and one draw needn't show every extreme that they name: `page_table`: A permutation: entry p * 64 + j is the physical page that holds logical page j of prompt p; physical page r is rows r * 128 to (r + 1) * 128 - 1 of prompt_states. `sample_order`: A permutation; completion i continues prompt sample_order[i] // 32.
All inputs are finite; a program needn't handle non-finite values.
Results may differ from a plain program's by a relative error of at most 0.034.
Values may be sent and summed in bfloat16 or wider, within the bound.
A program may use at most 128 MiB of HBM per device.

v0:
```python
import jax
import jax.numpy as jnp
from jax import lax
from jax.sharding import PartitionSpec as P

D = 8192
HEAD_DIM = 128
KV_HEADS = 4
GQA = 8
PAGE = 128
PROMPT_PAGES = 64


rope_base = 1000000.0


def rotate(vector, position):
    half_dim = vector.shape[-1] // 2
    frequency = rope_base ** (-jnp.arange(half_dim, dtype=jnp.float32) * 2.0 / vector.shape[-1])
    angles = position.astype(jnp.float32)[..., None] * frequency
    cosine = jnp.cos(angles)
    sine_part = jnp.sin(angles)
    first_half = vector[..., :half_dim]
    second_half = vector[..., half_dim:]
    return jnp.concatenate(
        [
            first_half * cosine - second_half * sine_part,
            second_half * cosine + first_half * sine_part,
        ],
        axis=-1,
    )


def finish_heads(prefix_top, prefix_total, prefix_sum, queries, new_keys, new_values):
    score_scale = queries.shape[-1] ** (-0.5)
    query_wide = queries.astype(jnp.float32)
    key_wide = new_keys.astype(jnp.float32)
    value_wide = new_values.astype(jnp.float32)
    own_score = jnp.sum(query_wide * key_wide, axis=-1) * score_scale
    back_score = jnp.sum(query_wide[1] * key_wide[0], axis=-1) * score_scale
    first_high = jnp.maximum(prefix_top[0], own_score[0])
    first_old = jnp.exp(prefix_top[0] - first_high)
    first_own = jnp.exp(own_score[0] - first_high)
    first_out = (first_old[..., None] * prefix_sum[0] + first_own[..., None] * value_wide[0]) / (
        first_old * prefix_total[0] + first_own
    )[..., None]
    second_high = jnp.maximum(jnp.maximum(prefix_top[1], own_score[1]), back_score)
    second_old = jnp.exp(prefix_top[1] - second_high)
    second_back = jnp.exp(back_score - second_high)
    second_own = jnp.exp(own_score[1] - second_high)
    second_num = (
        second_old[..., None] * prefix_sum[1]
        + second_back[..., None] * value_wide[0]
        + second_own[..., None] * value_wide[1]
    )
    second_out = second_num / (second_old * prefix_total[1] + second_back + second_own)[..., None]
    return jnp.stack([first_out, second_out]).astype(jnp.bfloat16)


def on_device(
    prompt_states,
    page_table,
    step_states,
    sample_order,
    key_weight,
    value_weight,
    query_weight,
    out_weight,
):
    devices = lax.axis_size("sample")
    own_index = lax.axis_index("sample")
    row_count = prompt_states.shape[0]
    pages_here = row_count // PAGE
    heads_here = query_weight.shape[1] // HEAD_DIM
    total_pages = page_table.shape[0]
    prompts = total_pages // PROMPT_PAGES
    samples = sample_order.shape[0]
    group_size = samples // prompts
    score_scale = HEAD_DIM ** (-0.5)
    own_kv = own_index * heads_here // GQA
    slot_of = (
        jnp.zeros((total_pages,), jnp.int32)
        .at[page_table]
        .set(jnp.arange(total_pages, dtype=jnp.int32))
    )
    local_slots = lax.dynamic_slice_in_dim(slot_of, own_index * pages_here, pages_here)
    positions = (local_slots % PROMPT_PAGES * PAGE)[:, None] + jnp.arange(PAGE, dtype=jnp.int32)[
        None, :
    ]
    positions = positions.reshape(row_count)
    wide_states = step_states.reshape(2 * samples, D)
    key_piece = lax.all_gather(key_weight, "sample", axis=0, tiled=True)
    value_piece = lax.all_gather(value_weight, "sample", axis=0, tiled=True)
    piece_rows = key_piece.shape[0]
    key_acc = jnp.einsum(
        "rn,nkd->krd",
        prompt_states,
        key_piece.reshape(piece_rows, KV_HEADS, HEAD_DIM),
        preferred_element_type=jnp.float32,
    )
    value_acc = jnp.einsum(
        "rn,nkd->krd",
        prompt_states,
        value_piece.reshape(piece_rows, KV_HEADS, HEAD_DIM),
        preferred_element_type=jnp.float32,
    )
    key_head = lax.dynamic_slice_in_dim(key_piece, own_kv * HEAD_DIM, HEAD_DIM, 1)
    value_head = lax.dynamic_slice_in_dim(value_piece, own_kv * HEAD_DIM, HEAD_DIM, 1)
    key_step = jnp.dot(wide_states, key_head, preferred_element_type=jnp.float32)
    value_step = jnp.dot(wide_states, value_head, preferred_element_type=jnp.float32)
    key_acc, value_acc, key_step, value_step = (key_acc, value_acc, key_step, value_step)
    page_keys = rotate(key_acc, positions[None, :]).astype(jnp.bfloat16)
    page_values = value_acc.astype(jnp.bfloat16)
    step_place = (PROMPT_PAGES * PAGE + jnp.arange(2, dtype=jnp.int32))[:, None, None]
    queries = jnp.dot(wide_states, query_weight, preferred_element_type=jnp.float32).reshape(
        2, samples, heads_here, HEAD_DIM
    )
    queries = rotate(queries, step_place).astype(jnp.bfloat16)
    new_keys = rotate(key_step.reshape(2, samples, HEAD_DIM), step_place[:, :, 0]).astype(
        jnp.bfloat16
    )
    new_values = value_step.reshape(2, samples, HEAD_DIM).astype(jnp.bfloat16)
    inverse = (
        jnp.zeros((samples,), jnp.int32).at[sample_order].set(jnp.arange(samples, dtype=jnp.int32))
    )
    spread = devices // KV_HEADS
    send_keys = jnp.repeat(page_keys, spread, axis=0)
    send_values = jnp.repeat(page_values, spread, axis=0)
    all_keys, all_values = (
        lax.all_to_all(send_keys, "sample", split_axis=0, concat_axis=1, tiled=True),
        lax.all_to_all(send_values, "sample", split_axis=0, concat_axis=1, tiled=True),
    )
    logical = page_table.reshape(prompts, PROMPT_PAGES)
    all_keys = all_keys.reshape(total_pages, PAGE, HEAD_DIM)[logical].reshape(
        prompts, PROMPT_PAGES * PAGE, HEAD_DIM
    )
    all_values = all_values.reshape(total_pages, PAGE, HEAD_DIM)[logical].reshape(
        prompts, PROMPT_PAGES * PAGE, HEAD_DIM
    )
    sorted_query = queries[:, inverse].reshape(2, prompts, group_size, heads_here, HEAD_DIM)
    scores = (
        jnp.einsum("spmhd,pld->spmhl", sorted_query, all_keys, preferred_element_type=jnp.float32)
        * score_scale
    )
    prefix_top = jnp.max(scores, axis=-1)
    weights = jnp.exp(scores - prefix_top[..., None])
    prefix_total = jnp.sum(weights, axis=-1)
    prefix_sum = jnp.einsum(
        "spmhl,pld->spmhd",
        weights.astype(jnp.bfloat16),
        all_values,
        preferred_element_type=jnp.float32,
    )
    prefix_top = prefix_top.reshape(2, samples, heads_here)[:, sample_order]
    prefix_total = prefix_total.reshape(2, samples, heads_here)[:, sample_order]
    prefix_sum = prefix_sum.reshape(2, samples, heads_here, HEAD_DIM)[:, sample_order]
    head_out = finish_heads(
        prefix_top,
        prefix_total,
        prefix_sum,
        queries,
        new_keys[:, :, None, :],
        new_values[:, :, None, :],
    )
    flat_heads = head_out.reshape(2, samples, heads_here * HEAD_DIM)
    head_terms = jnp.einsum(
        "srk,kd->srd", flat_heads, out_weight, preferred_element_type=jnp.float32
    )
    return lax.psum_scatter(
        head_terms.astype(jnp.bfloat16), "sample", scatter_dimension=2, tiled=True
    )


def solution(mesh):
    in_specs = (
        P(("groups", "sample"), None),
        P("groups"),
        P(None, "groups", None),
        P("groups"),
        P("sample", None),
        P("sample", None),
        P(None, "sample"),
        P("sample", None),
    )
    out_specs = P(None, "groups", "sample")
    return jax.shard_map(
        on_device, mesh=mesh, in_specs=in_specs, out_specs=out_specs, check_vma=False
    )
```

profile of v0, /device:TPU:0, one launch (start us, length us, event | category | flops | bytes accessed | tf_op | source)
XLA Modules:
  0.0 351.2 jit_solution(6273337491218514646)
XLA Ops:
  6.5 0.7 all-gather.3.cloned.1.call-update
  7.3 0.0 all-gather.5.cloned.1.call-start
  7.3 0.7 all-gather.5.cloned.1.call-update
  8.0 0.7 compare_select_fusion.2
  8.7 0.8 scatter_custom_fusion
  9.5 0.1 fusion.61
  9.6 0.1 convert_bitcast_fusion
  9.6 0.5 multiply_cosine_fusion
  10.2 77.0 %all-gather.3.cloned.1.call-done = bf16[8192,512]{1,0:T(8,128)(2,1)} async-done(((bf16[512,512]{1,0:T(8,128)(2,1)}), bf16[8192,512]{1,0:T(8,128)(2,1)}) %all-gather.3.cloned.1.call-update) | async-done | bytes 8388624 | tf_op jit(solution)/shard_map/all_gather | solution.py:92
  87.2 11.5 %copy.36 = bf16[8192,512]{0,1:T(8,128)(2,1)} copy(bf16[8192,512]{1,0:T(8,128)(2,1)} %all-gather.3.cloned.1.call-done) | data formatting | bytes 16777216 | tf_op jit(solution)/shard_map/all_gather | solution.py:92
  98.6 9.5 %fusion.16 = f32[4,512,128]{1,2,0:T(8,128)S(1)} fusion(bf16[8192,4,128]{0,2,1:T(8,128)(2,1)} %bitcast.153, bf16[512,8192]{1,0:T(8,128)(2,1)} %param.8), kind=kOutput, calls=%fused_computation.26 | convolution fusion | flops 4294967296 | bytes 17825792 | tf_op jit(solution)/shard_map/rn,nkd->krd/dot_general | solution.py:95
  108.2 0.2 subtract_convert_fusion
  108.4 0.3 copy.37
  108.7 1.8 broadcast_in_dim.13
  110.5 3.7 %all-to-all-start = ((bf16[16,512,128]{2,1,0:T(8,128)(2,1)}), bf16[16,512,128]{2,1,0:T(8,128)(2,1)S(1)}, u32[]{:S(2)}, u32[]{:S(2)}) async-start(bf16[16,512,128]{2,1,0:T(8,128)(2,1)} %bitcast.4), calls=%async_computation | async-start | bytes 4194304 | tf_op jit(solution)/shard_map/all_to_all | solution.py:130
  114.2 6.4 %copy.61 = bf16[256,8192]{1,0:T(8,128)(2,1)} copy(bf16[256,8192]{0,1:T(8,128)(2,1)} %bitcast.158) | data formatting | bytes 8388608 | tf_op jit(solution)/shard_map/dot_general | solution.py:115
  120.6 0.1 multiply_cosine_fusion.1
  120.7 4.3 %fusion.37 = f32[2,32,2,128]{3,1,2,0:T(8,128)S(1)} fusion(bf16[2,128,8192,1]{2,1,0,3:T(8,128)(2,1)} %bitcast.152, bf16[2,32,8192]{2,1,0:T(8,128)(2,1)S(1)} %copy-done), kind=kOutput, calls=%fused_computation.33 | convolution fusion | flops 268435456 | bytes 5308416 | tf_op jit(solution)/shard_map/dot_general | solution.py:115
  125.1 69.1 %all-gather.5.cloned.1.call-done = bf16[8192,512]{1,0:T(8,128)(2,1)} async-done(((bf16[512,512]{1,0:T(8,128)(2,1)}), bf16[8192,512]{1,0:T(8,128)(2,1)}) %all-gather.5.cloned.1.call-update) | async-done | bytes 8388624 | tf_op jit(solution)/shard_map/all_gather | solution.py:93
  194.2 11.4 %copy.44 = bf16[8192,512]{0,1:T(8,128)(2,1)} copy(bf16[8192,512]{1,0:T(8,128)(2,1)} %all-gather.5.cloned.1.call-done) | data formatting | bytes 16777216 | tf_op jit(solution)/shard_map/all_gather | solution.py:93
  205.6 11.1 %fusion.22 = bf16[4,512,128]{1,2,0:T(8,128)(2,1)} fusion(bf16[8192,4,128]{0,2,1:T(8,128)(2,1)} %bitcast.154, bf16[512,8192]{1,0:T(8,128)(2,1)} %param.8), kind=kOutput, calls=%fused_computation.28 | convolution fusion | flops 4295229440 | bytes 17301504 | tf_op jit(solution)/shard_map/rn,nkd->krd/dot_general | solution.py:101
  216.7 2.1 copy.45
  218.7 0.0 all-to-all-done
  218.7 2.8 broadcast_in_dim.17
  221.6 7.3 %all-to-all-start.1 = ((bf16[16,512,128]{2,1,0:T(8,128)(2,1)}), bf16[16,512,128]{2,1,0:T(8,128)(2,1)}, u32[]{:S(2)}, u32[]{:S(2)}) async-start(bf16[16,512,128]{2,1,0:T(8,128)(2,1)} %bitcast.26), calls=%async_computation.1 | async-start | bytes 4194304 | tf_op jit(solution)/shard_map/all_to_all | solution.py:131
  228.9 0.0 reduce-scatter.2.cloned.1.call-start
  228.9 0.1 subtract_convert_fusion.1
  229.0 0.1 fusion.73
  229.2 0.9 scatter_custom_fusion.1
  230.1 0.6 gather_fusion.1
  230.7 2.1 fusion.14
  232.8 0.1 subtract_convert_fusion.2
  232.9 0.1 fusion.53
  233.0 0.1 maximum_convert_fusion
  233.1 0.1 fusion.43
  233.2 0.1 multiply_reduce_fusion
  233.3 2.1 fusion.34
  235.4 2.1 gather_fusion
  237.5 4.2 %fusion.77 = (f32[2,32,2]{1,2,0:T(2,128)S(1)}, f32[2,1,32,2,8192]{4,2,3,0,1:T(8,128)}) fusion(bf16[8192,128,1,1]{1,0,3,2:T(8,128)(2,1)} %bitcast.156, bf16[2,32,2,128]{3,2,0,1:T(2,128)(2,1)S(1)} %bitcast.163), kind=kOutput, calls=%fused_computation.111 | convolution fusion | flops 270532480 | bytes 6324736 | tf_op jit(solution)/shard_map/spmhd,pld->spmhl/dot_general | solution.py:142
  241.8 0.1 copy.41
  241.9 2.9 fusion.6
  244.8 0.1 copy.48
  244.9 0.6 gather_fusion.5
  245.5 0.1 copy.49
  245.6 0.1 copy.56
  245.7 0.6 gather_fusion.2
  246.4 0.1 copy.42
  246.4 0.1 copy.51
  246.5 0.1 copy.43
  246.6 0.1 copy.47
  246.7 0.1 copy.50
  246.8 0.1 copy.53
  246.9 0.1 copy.54
  247.0 0.1 copy.55
  247.1 0.1 copy.57
  247.1 22.9 %all-to-all-done.1 = bf16[16,512,128]{2,1,0:T(8,128)(2,1)} async-done(((bf16[16,512,128]{2,1,0:T(8,128)(2,1)}), bf16[16,512,128]{2,1,0:T(8,128)(2,1)}, u32[]{:S(2)}, u32[]{:S(2)}) %all-to-all-start.1) | async-done | bytes 2097184 | tf_op jit(solution)/shard_map/all_to_all | solution.py:131
  270.0 2.5 gather_fusion.3
  272.6 3.0 fusion.25
  275.6 0.1 copy.46
  275.6 0.6 gather_fusion.4
  276.3 0.3 fusion.50
  276.7 4.0 %convolution_convert_fusion = bf16[2,32,8192]{2,1,0:T(8,128)(2,1)} fusion(bf16[256,8192]{1,0:T(8,128)(2,1)} %param.15, bf16[1,32,256]{2,1,0:T(8,128)(2,1)S(1)} %stack.10, bf16[1,32,256]{2,1,0:T(8,128)(2,1)S(1)} %stack.9), kind=kOutput, calls=%fused_computation.10 | convolution fusion | flops 268976128 | bytes 5275648 | tf_op jit(solution)/shard_map/srk,kd->srd/dot_general | solution.py:166
  280.7 0.0 reduce-scatter.2.cloned.1.call-update
  280.7 64.0 %reduce-scatter.2.cloned.1.call-done = bf16[2,32,512]{2,1,0:T(8,128)(2,1)} async-done(((bf16[2,32,8192]{2,1,0:T(8,128)(2,1)}), bf16[2,32,512]{2,1,0:T(8,128)(2,1)}) %reduce-scatter.2.cloned.1.call-update) | async-done | bytes 65552 | tf_op jit(solution)/shard_map/reduce_scatter | solution.py:169
  (23 shorter events, 0.2 us)
Async XLA Ops:
  6.5 114.2 %copy-start = (bf16[2,32,8192]{2,1,0:T(8,128)(2,1)S(1)}, bf16[2,32,8192]{2,1,0:T(8,128)(2,1)}, u32[]{:S(2)}) copy-start(bf16[2,32,8192]{2,1,0:T(8,128)(2,1)} %param.10) | copy-start | bytes 3145732
  6.5 80.6 %all-gather.3.cloned.1.call-start = ((), (), s32[]{:S(2)}) async-start(), calls=%async_computation.3 | async-start | bytes 8912896 | tf_op jit(solution)/shard_map/all_gather | solution.py:92
  7.3 186.9 %all-gather.5.cloned.1.call-start = ((), (), s32[]{:S(2)}) async-start(), calls=%async_computation.4 | async-start | bytes 8912896 | tf_op jit(solution)/shard_map/all_gather | solution.py:93
  110.5 108.3 %all-to-all-start = ((bf16[16,512,128]{2,1,0:T(8,128)(2,1)}), bf16[16,512,128]{2,1,0:T(8,128)(2,1)S(1)}, u32[]{:S(2)}, u32[]{:S(2)}) async-start(bf16[16,512,128]{2,1,0:T(8,128)(2,1)} %bitcast.4), calls=%async_computation | async-start | bytes 4194304 | tf_op jit(solution)/shard_map/all_to_all | solution.py:130
  216.7 12.5 %copy-start.1 = (s32[32]{0:T(128)S(1)}, s32[32]{0:T(128)}, u32[]{:S(2)}) copy-start(s32[32]{0:T(128)} %param.11) | copy-start | bytes 388
  221.6 48.4 %all-to-all-start.1 = ((bf16[16,512,128]{2,1,0:T(8,128)(2,1)}), bf16[16,512,128]{2,1,0:T(8,128)(2,1)}, u32[]{:S(2)}, u32[]{:S(2)}) async-start(bf16[16,512,128]{2,1,0:T(8,128)(2,1)} %bitcast.26), calls=%async_computation.1 | async-start | bytes 4194304 | tf_op jit(solution)/shard_map/all_to_all | solution.py:131
  228.9 115.8 %reduce-scatter.2.cloned.1.call-start = ((), (), s32[]{:S(2)}) async-start(), calls=%async_computation.5 | async-start | bytes 1114112 | tf_op jit(solution)/shard_map/reduce_scatter | solution.py:169
Sparse Core Ops, SparseCore 0:
  9.5 77.5 all-gather.2
  89.3 104.7 all-gather.4
  280.8 63.8 reduce-scatter.1
where the time goes:
time: 352 us; the launch traced here: 351 us
  waiting for transfers between devices  234 us (66%)
  local copies, waits for them, and re-layouts  46.4 us (13%)
  matrix products  40.4 us (11%)
  between operations  13.4 us (4%)
  starting transfers between devices  11.1 us (3%)
  other arithmetic  5.57 us (2%)
    all_gather x1, waiting for transfers between devices, on_device(): key_piece = lax.all_gather(key_weight, 'sample', axis=0, tiled=True)  77 us
    all_gather x1, waiting for transfers between devices, on_device(): value_piece = lax.all_gather(value_weight, 'sample', axis=0, tiled=True)  69.1 us
    reduce_scatter x1, waiting for transfers between devices, on_device(): lax.psum_scatter(head_terms.astype(jnp.bfloat16), 'sample', scatter_dimen...  64 us
    all_to_all x1, waiting for transfers between devices, on_device(): lax.all_to_all(send_values, 'sample', split_axis=0, concat_axis=1, tiled=...  22.9 us
    all_gather x1, local copies, waits for them, and re-layouts, on_device(): key_piece = lax.all_gather(key_weight, 'sample', axis=0, tiled=True)  11.5 us
    all_gather x1, local copies, waits for them, and re-layouts, on_device(): value_piece = lax.all_gather(value_weight, 'sample', axis=0, tiled=True)  11.4 us
    dot_general x1, matrix products, on_device(): jnp.einsum('rn,nkd->krd', prompt_states, value_piece.reshape(piece_rows,...  11.1 us
    dot_general x1, matrix products, on_device(): jnp.einsum('rn,nkd->krd', prompt_states, key_piece.reshape(piece_rows, KV...  9.54 us
  transfers between devices with their start and end apart: 5, of which 4 were waited for; matrix products, arithmetic and copies ran while one was open for 22% of the time, Pallas kernels for 0%

commit v1 on v0

v1 whole, which is shorter than its diff:
```python
import functools

import jax
import jax.numpy as jnp
from jax import lax
from jax.experimental import pallas as pl
from jax.experimental.pallas import tpu as pltpu
from jax.sharding import PartitionSpec as P

HEAD_DIM = 128
KV_HEADS = 4
GQA = 8
PAGE = 128
PROMPT_PAGES = 64
HALF = KV_HEADS // 2 * HEAD_DIM
LOW = -1e30
TAIL = 16
MESH = pl.DeviceIdType.MESH
ROPE_BASE = 1000000.0


def flip(value, bits):
    result, weight = value, 1
    while weight <= bits:
        if bits & weight:
            result = result + weight * (1 - 2 * lax.rem(lax.div(value, weight), 2))
        weight *= 2
    return result


def turn(value, cosine, sine):
    return value * cosine + pltpu.roll(value, HEAD_DIM // 2, 1) * sine


def kernel(cfg, *refs):
    groups, devices, near, samples, heads, masked = cfg
    (states, step, wk, wv, wq, wo, cosine, sine) = refs[:8]
    refs = refs[8:]
    if masked:
        token_prompt, query_prompt = refs[:2]
        refs = refs[2:]
    (out, st, wbuf, wqb, wob, acc, kb, vb, qown, qbuf, pout, pbuf, nk, nkr, tbuf, prbuf, sbuf, rbuf,
     load_sem, send_sem, wsem, st_sem, qsem, psem, nsem, pair_sem, rsem) = refs
    chips = devices // 2
    deep = chips // near
    rows = wk.shape[0]
    part = 2 * rows // groups
    own_parts = groups // 2
    tokens_here = states.shape[0]
    tokens = 2 * tokens_here
    wide = step.shape[0]
    dim = step.shape[1]
    cols = dim // devices
    half = devices // 2

    g = lax.axis_index("groups")
    me = lax.axis_index("sample")
    c = lax.rem(me, 2)
    p = lax.div(me, 2)
    y = lax.rem(p, near)
    z = lax.div(p, near)
    mate = p * 2 + 1 - c
    kv = lax.div(me * heads, GQA)
    kv_core = lax.div(kv, 2)
    kv_slot = lax.rem(kv, 2)

    def aligned(value, step_size):
        return pl.multiple_of(value, step_size)

    my_rows = pl.ds(aligned(c * tokens_here, tokens_here), tokens_here)
    loads = [
        pltpu.make_async_copy(step, st.at[pl.ds(tokens, wide)], load_sem.at[0]),
        pltpu.make_async_copy(wq, wqb, load_sem.at[1]),
        pltpu.make_async_copy(states, st.at[my_rows], load_sem.at[2]),
        pltpu.make_async_copy(wo, wob, load_sem.at[3]),
    ]
    own_w = pl.ds(aligned(me * rows, rows), rows)
    own_cols = pl.ds(aligned(c * HALF, HALF), HALF)
    loads.append(
        pltpu.make_async_copy(wk.at[:, own_cols], wbuf.at[own_w, pl.ds(0, HALF)], load_sem.at[4])
    )
    loads.append(
        pltpu.make_async_copy(wv.at[:, own_cols], wbuf.at[own_w, pl.ds(HALF, HALF)], load_sem.at[5])
    )
    for load in loads:
        load.start()

    barrier = pltpu.get_barrier_semaphore()
    for k in range(1, devices):
        pl.semaphore_signal(
            barrier, inc=1, device_id=(g, flip(me, k)), device_id_type=MESH
        )
    for k in range(1, groups):
        pl.semaphore_signal(
            barrier, inc=1, device_id=(lax.rem(g + k, groups), me), device_id_type=MESH
        )
    pl.semaphore_wait(barrier, devices + groups - 2)

    sends = []

    def send(src, dst, sem, target, when=None):
        copy = pltpu.make_async_remote_copy(
            src_ref=src, dst_ref=dst, send_sem=send_sem.at[len(sends)], recv_sem=sem,
            device_id=target, device_id_type=MESH,
        )
        if when is None:
            copy.start()
        else:
            pl.when(when)(copy.start)
        sends.append((copy, when))

    def w_rows(block):
        return pl.ds(aligned(block * part, part), part)

    def send_own(src_row, block, core, target, when=None):
        src_rows = pl.ds(src_row, part)
        src_cols = pl.ds(aligned(core * HALF, HALF), HALF)
        send(wk.at[src_rows, src_cols], wbuf.at[w_rows(block), pl.ds(0, HALF)],
             wsem.at[block], target, when)
        send(wv.at[src_rows, src_cols], wbuf.at[w_rows(block), pl.ds(HALF, HALF)],
             wsem.at[block], target, when)

    def w_wait(block):
        view = wbuf.at[w_rows(block)]
        pltpu.make_async_copy(view, view, wsem.at[block]).wait()

    owner = lax.div(g, own_parts)
    line_row = aligned(lax.rem(g, own_parts) * part, part)
    line_block = p * groups + g
    for k in range(1, deep):
        chip = flip(z, k) * near + y
        for core in range(2):
            send_own(line_row, line_block, core, (g, chip * 2 + core), c == owner)
    for h in range(own_parts):
        block = p * groups + c * own_parts + h
        for k in range(1, near):
            chip = z * near + flip(y, k)
            for core in range(2):
                send_own(h * part, block, core, (g, chip * 2 + core))
        send_own(h * part, block, 1 - c, (g, mate))
    send(states, st.at[my_rows], st_sem, (g, mate))

    loads[0].wait()
    loads[1].wait()
    depth = 1024

    def q_step(i, total):
        at = pl.ds(aligned(i * depth, depth), depth)
        return total + jnp.dot(
            st[pl.ds(tokens, wide), at], wqb[at, :], preferred_element_type=jnp.float32
        )

    queries = lax.fori_loop(
        0, dim // depth, q_step, jnp.zeros((wide, heads * HEAD_DIM), jnp.float32)
    )
    step_cos = cosine[pl.ds(tokens, wide), :]
    step_sin = sine[pl.ds(tokens, wide), :]
    for h in range(heads):
        one = queries[:, h * HEAD_DIM : (h + 1) * HEAD_DIM]
        qown[pl.ds(h * wide, wide), :] = turn(one, step_cos, step_sin).astype(jnp.bfloat16)

    def give(src, dst, sem, target):
        send(src, dst, sem, (g, target), target != me)

        @pl.when(target == me)
        def _():
            pltpu.make_async_copy(src, dst, sem).start()

    q_slot = lax.rem(me, half)
    for k in range(chips):
        give(qown, qbuf.at[q_slot], qsem.at[q_slot], flip(p, k) * 2 + kv_core)

    def cross(block):
        view = wbuf.at[w_rows(block)]
        for k in range(1, groups):
            send(view, view, wsem.at[block], (lax.rem(g + k, groups), me))

    def second(k):
        for j in range(1, near):
            block = (flip(z, k) * near + flip(y, j)) * groups + g
            w_wait(block)
            cross(block)

    for k in range(1, deep):
        block = (flip(z, k) * near + y) * groups + g
        w_wait(block)
        view = wbuf.at[w_rows(block)]
        for j in range(1, near):
            send(view, view, wsem.at[block],
                 (g, (z * near + flip(y, j)) * 2 + c))
        cross(block)
        if k > 1:
            second(k - 1)
    second(deep - 1)

    total_rows = tokens + wide
    tiles = 4
    tile = total_rows // tiles

    def multiply(chip, first):
        at = pl.ds(aligned(chip * 2 * rows, 2 * rows), 2 * rows)

        @pl.loop(0, tiles)
        def _(i):
            here = pl.ds(aligned(i * tile, tile), tile)
            value = jnp.dot(st[here, at], wbuf[at, :], preferred_element_type=jnp.float32)
            if first:
                acc[here, :] = value
            else:
                acc[here, :] += value

    loads[2].wait()
    loads[4].wait()
    loads[5].wait()
    other_rows = st.at[pl.ds(aligned((1 - c) * tokens_here, tokens_here), tokens_here)]
    pltpu.make_async_copy(other_rows, other_rows, st_sem).wait()
    for h in range(own_parts):
        w_wait(p * groups + (1 - c) * own_parts + h)
    multiply(p, True)
    for j in range(1, near):
        chip = z * near + flip(y, j)
        for h in range(groups):
            w_wait(chip * groups + h)
        multiply(chip, False)
    for k in range(1, deep):
        for j in range(near):
            chip = flip(z, k) * near + flip(y, j)
            for h in range(1, groups):
                w_wait(chip * groups + lax.rem(g + h, groups))
            multiply(chip, False)

    for j in range(2):
        key = acc[:, j * HEAD_DIM : (j + 1) * HEAD_DIM]
        kb[j] = turn(key, cosine[...], sine[...]).astype(jnp.bfloat16)
        vb[j] = acc[:, HALF + j * HEAD_DIM : HALF + (j + 1) * HEAD_DIM].astype(jnp.bfloat16)
    nk[0] = kb[kv_slot, pl.ds(tokens, wide), :]
    nk[1] = vb[kv_slot, pl.ds(tokens, wide), :]
    send(nk, nkr, nsem, (g, mate))

    scale = HEAD_DIM ** (-0.5)
    for t in range(half):
        pltpu.make_async_copy(qbuf.at[t], qbuf.at[t], qsem.at[t]).wait()
    lanes = heads * wide
    pair = 2
    for t in range(0, half, pair):
        j = t // (half // 2)
        query = qbuf[pl.ds(t, pair)].reshape(pair * lanes, HEAD_DIM)
        scores = lax.dot_general(
            kb[j, pl.ds(0, tokens), :], query, (((1,), (1,)), ((), ())),
            preferred_element_type=jnp.float32,
        ) * scale
        if masked:
            prompt_row = jnp.concatenate([query_prompt[...]] * pair, axis=1)
            allowed = token_prompt[...] == prompt_row
            scores = jnp.where(allowed, scores, LOW)
        top = jnp.max(scores, axis=0, keepdims=True)
        weights = jnp.exp(scores - top)
        if masked:
            weights = jnp.where(allowed, weights, 0.0)
        total = jnp.sum(weights, axis=0, keepdims=True)
        value = lax.dot_general(
            vb[j, pl.ds(0, tokens), :], weights.astype(jnp.bfloat16), (((0,), (0,)), ((), ())),
            preferred_element_type=jnp.float32,
        )
        if masked:
            total = jnp.maximum(total, 1e-30)
        value = value / total
        mass = top + jnp.log(total)
        high = mass.astype(jnp.bfloat16).astype(jnp.float32)
        rest = mass - high
        middle = rest.astype(jnp.bfloat16).astype(jnp.float32)
        low = rest - middle
        row = lax.broadcasted_iota(jnp.int32, (TAIL, pair * lanes), 0)
        tail = jnp.where(row == 0, high, jnp.where(row == 1, middle, low))
        for u in range(pair):
            at = slice(u * lanes, (u + 1) * lanes)
            pout[t + u, pl.ds(0, HEAD_DIM), :] = value[:, at].astype(jnp.bfloat16)
            pout[t + u, pl.ds(HEAD_DIM, TAIL), :] = tail[:, at].astype(jnp.bfloat16)
        for u in range(pair):
            give(pout.at[t + u], pbuf.at[p], psem.at[p], c * half + t + u)

    pltpu.make_async_copy(nkr, nkr, nsem).wait()
    mine = kv_core == c
    new_key = jnp.where(mine, nk[0].astype(jnp.float32), nkr[0].astype(jnp.float32))
    new_value = jnp.where(mine, nk[1].astype(jnp.float32), nkr[1].astype(jnp.float32))

    def spread(value):
        return jnp.concatenate([value] * heads, axis=0)

    def earlier(value):
        return spread(jnp.concatenate([value[:samples], value[:samples]], axis=0))

    wide_query = qown[...].astype(jnp.float32)
    own = jnp.sum((wide_query * spread(new_key)).T, axis=0, keepdims=True) * scale
    back = jnp.sum((wide_query * earlier(new_key)).T, axis=0, keepdims=True) * scale
    lane = lax.broadcasted_iota(jnp.int32, (1, lanes), 1)
    late = lax.rem(lane, wide) >= samples
    back = jnp.where(late, back, LOW)
    high = jnp.maximum(own, back)
    masses = []
    for s in range(chips):
        pltpu.make_async_copy(pbuf.at[s], pbuf.at[s], psem.at[s]).wait()
    for s in range(chips):
        tail = pbuf[s, pl.ds(HEAD_DIM, TAIL), :].astype(jnp.float32)
        masses.append(tail[0:1] + tail[1:2] + tail[2:3])
        high = jnp.maximum(high, masses[-1])
    own = jnp.exp(own - high)
    back = jnp.where(late, jnp.exp(back - high), 0.0)
    below = own + back
    above = own * spread(new_value).T + back * earlier(new_value).T
    for s in range(chips):
        weight = jnp.exp(masses[s] - high)
        below += weight
        above += weight * pbuf[s, pl.ds(0, HEAD_DIM), :].astype(jnp.float32)
    head_out = (above / below).T
    flat = jnp.concatenate(
        [head_out[h * wide : (h + 1) * wide] for h in range(heads)], axis=1
    ).astype(jnp.bfloat16)

    loads[3].wait()

    def term(target):
        at = pl.ds(aligned(target * cols, cols), cols)
        return jnp.dot(flat, wob[:, at], preferred_element_type=jnp.float32)

    for k in reversed(range(chips)):
        chip = flip(p, k)
        tbuf[chip] = term(chip * 2 + 1 - c).astype(jnp.bfloat16)
        send(tbuf.at[chip], prbuf.at[chip], pair_sem.at[chip], (g, mate))
    for k in reversed(range(chips)):
        chip = flip(p, k)
        value = term(chip * 2 + c)
        pltpu.make_async_copy(prbuf.at[chip], prbuf.at[chip], pair_sem.at[chip]).wait()
        value = value + prbuf[chip].astype(jnp.float32)
        if k:
            sbuf[chip] = value.astype(jnp.bfloat16)
            send(sbuf.at[chip], rbuf.at[p], rsem.at[p], (g, chip * 2 + c))
        else:
            result = value
    for k in range(1, chips):
        chip = flip(p, k)
        pltpu.make_async_copy(rbuf.at[chip], rbuf.at[chip], rsem.at[chip]).wait()
        result = result + rbuf[chip].astype(jnp.float32)
    out[...] = result.astype(jnp.bfloat16)
    assert len(sends) == send_sem.shape[0]
    for copy, when in sends:
        if when is None:
            copy.wait_send()
        else:
            pl.when(when)(copy.wait_send)


def on_device(
    near,
    prompt_states,
    page_table,
    step_states,
    sample_order,
    key_weight,
    value_weight,
    query_weight,
    out_weight,
):
    groups = lax.axis_size("groups")
    devices = lax.axis_size("sample")
    chips = devices // 2
    own_chip = lax.axis_index("sample") // 2
    dim = prompt_states.shape[1]
    tokens = 2 * prompt_states.shape[0]
    chip_pages = tokens // PAGE
    heads = query_weight.shape[1] // HEAD_DIM
    total_pages = page_table.shape[0]
    prompts = total_pages // PROMPT_PAGES
    samples = sample_order.shape[0]
    wide = 2 * samples
    cols = dim // devices
    half = devices // 2
    lanes = heads * wide

    page_ids = own_chip * chip_pages + jnp.arange(chip_pages, dtype=jnp.int32)
    slots = jnp.sum(
        jnp.where(
            page_table[None, :] == page_ids[:, None],
            jnp.arange(total_pages, dtype=jnp.int32)[None, :],
            0,
        ),
        axis=1,
    )
    place = (slots % PROMPT_PAGES * PAGE)[:, None] + jnp.arange(PAGE, dtype=jnp.int32)[None, :]
    later = PROMPT_PAGES * PAGE + jnp.repeat(jnp.arange(2, dtype=jnp.int32), samples)
    position = jnp.concatenate([place.reshape(tokens), later]).astype(jnp.float32)
    lane = jnp.arange(HEAD_DIM, dtype=jnp.int32)
    order = (lane % (HEAD_DIM // 2)).astype(jnp.float32)
    frequency = ROPE_BASE ** (-order * 2.0 / HEAD_DIM)
    angle = position[:, None] * frequency[None, :]
    cosine = jnp.cos(angle)
    sine = jnp.where(lane < HEAD_DIM // 2, -1.0, 1.0)[None, :] * jnp.sin(angle)

    deep = chips // near
    send_count = (
        4 * (deep - 1)
        + groups // 2 * (4 * (near - 1) + 2)
        + (deep - 1) * (near - 1 + near * (groups - 1))
        + 3 * chips
        + half
        + 1
    )
    masked = prompts > 1
    args = [
        prompt_states,
        step_states.reshape(wide, dim),
        key_weight,
        value_weight,
        query_weight,
        out_weight,
        cosine,
        sine,
    ]
    specs = [pl.BlockSpec(memory_space=pl.ANY)] * 6 + [pl.BlockSpec(memory_space=pltpu.VMEM)] * 2
    if masked:
        token_prompt = jnp.repeat(slots // PROMPT_PAGES, PAGE)[:, None]
        query_prompt = jnp.tile(sample_order // (samples // prompts), 2 * heads)[None, :]
        args += [token_prompt, query_prompt]
        specs += [pl.BlockSpec(memory_space=pltpu.VMEM)] * 2
    bf16, f32 = jnp.bfloat16, jnp.float32
    dma = pltpu.SemaphoreType.DMA
    result = pl.pallas_call(
        functools.partial(kernel, (groups, devices, near, samples, heads, masked)),
        out_shape=jax.ShapeDtypeStruct((wide, cols), bf16),
        in_specs=specs,
        out_specs=pl.BlockSpec(memory_space=pltpu.VMEM),
        scratch_shapes=[
            pltpu.VMEM((tokens + wide, dim), bf16),
            pltpu.VMEM((dim, 2 * HALF), bf16),
            pltpu.VMEM((dim, heads * HEAD_DIM), bf16),
            pltpu.VMEM((heads * HEAD_DIM, dim), bf16),
            pltpu.VMEM((tokens + wide, 2 * HALF), f32),
            pltpu.VMEM((2, tokens + wide, HEAD_DIM), bf16),
            pltpu.VMEM((2, tokens + wide, HEAD_DIM), bf16),
            pltpu.VMEM((lanes, HEAD_DIM), bf16),
            pltpu.VMEM((half, lanes, HEAD_DIM), bf16),
            pltpu.VMEM((half, HEAD_DIM + TAIL, lanes), bf16),
            pltpu.VMEM((chips, HEAD_DIM + TAIL, lanes), bf16),
            pltpu.VMEM((2, wide, HEAD_DIM), bf16),
            pltpu.VMEM((2, wide, HEAD_DIM), bf16),
            pltpu.VMEM((chips, wide, cols), bf16),
            pltpu.VMEM((chips, wide, cols), bf16),
            pltpu.VMEM((chips, wide, cols), bf16),
            pltpu.VMEM((chips, wide, cols), bf16),
            dma((6,)),
            dma((send_count,)),
            dma((chips * groups,)),
            dma,
            dma((half,)),
            dma((chips,)),
            dma,
            dma((chips,)),
            dma((chips,)),
        ],
        compiler_params=pltpu.CompilerParams(
            collective_id=0, has_side_effects=True, vmem_limit_bytes=60 * 1024 * 1024
        ),
        name="prefill_decode",
    )(*args)
    return result.reshape(2, samples, cols)


def solution(mesh):
    in_specs = (
        P(("groups", "sample"), None),
        P("groups"),
        P(None, "groups", None),
        P("groups"),
        P("sample", None),
        P("sample", None),
        P(None, "sample"),
        P("sample", None),
    )
    out_specs = P(None, "groups", "sample")
    near = 2 if mesh.shape["groups"] == 2 else 1
    return jax.shard_map(
        functools.partial(on_device, near), mesh=mesh, in_specs=in_specs, out_specs=out_specs,
        check_vma=False,
    )
```

time: 352 us -> 128 us (0.36)
  waiting for transfers between devices: 234 us -> 0 us
  Pallas kernels: 0 us -> 122 us
  local copies, waits for them, and re-layouts: 46.4 us -> 1.56 us
  matrix products: 40.4 us -> 0 us
  between operations: 13.4 us -> 0.01 us
  starting transfers between devices: 11.1 us -> 0 us
    all_gather x2 -> x0, waiting for transfers between devices: 146 us -> none  [the longest x1 77 us: on_device(): key_piece = lax.all_gather(key_weight, 'sample', axis=0, tiled=True)]
    pallas_call x0 -> x1, Pallas kernels: none -> 122 us  [on_device(): pl.pallas_call(functools.partial(kernel, (groups, devices, near, samples,...]
    reduce_scatter x1 -> x0, waiting for transfers between devices: 64 us -> none  [on_device(): lax.psum_scatter(head_terms.astype(jnp.bfloat16), 'sample', scatter_dimen...]
    dot_general x8 -> x0, matrix products: 40.4 us -> none  [the longest x1 11.1 us: on_device(): jnp.einsum('rn,nkd->krd', prompt_states, value_piece.reshape(piece_rows,...]
    all_gather x2 -> x0, local copies, waits for them, and re-layouts: 22.9 us -> none  [the longest x1 11.5 us: on_device(): key_piece = lax.all_gather(key_weight, 'sample', axis=0, tiled=True)]
    all_to_all x2 -> x0, waiting for transfers between devices: 22.9 us -> none  [the longest x1 22.9 us: on_device(): lax.all_to_all(send_values, 'sample', split_axis=0, concat_axis=1, tiled=...]
    all_to_all x2 -> x0, starting transfers between devices: 11 us -> none  [the longest x1 7.27 us: on_device(): lax.all_to_all(send_values, 'sample', split_axis=0, concat_axis=1, tiled=...]
    gather x6 -> x0, local copies, waits for them, and re-layouts: 7.19 us -> none  [the longest x1 2.54 us: on_device(): all_values.reshape(total_pages, PAGE, HEAD_DIM)[logical]]
  transfers between devices with their start and end apart: 5 -> 0, of which waited for: 4 -> 0; matrix products, arithmetic and copies ran while one was open for 22% -> 0% of each run, Pallas kernels for 0% -> 0%
where the time goes in v1:
time: 128 us
  Pallas kernels  122 us (95%)
  other arithmetic  4.09 us (3%)
  local copies, waits for them, and re-layouts  1.56 us (1%)
    pallas_call x1, Pallas kernels, on_device(): pl.pallas_call(functools.partial(kernel, (groups, devices, near, samples,...  122 us
    mul x1, other arithmetic, on_device(): sine = jnp.where(lane < HEAD_DIM // 2, -1.0, 1.0)[None, :] * jnp.sin(angle)  3.15 us

profile of v1, /device:TPU:0, one launch (start us, length us, event | category | flops | bytes accessed | tf_op | source)
XLA Modules:
  0.0 127.5 jit_solution(13807408023628560914)
XLA Ops:
  0.0 0.8 select_reduce_fusion
  0.9 0.1 add.70
  1.0 0.1 add_bitcast_fusion
  1.0 3.1 %fusion = (f32[1088,128]{1,0:T(8,128)}, f32[1088,128]{1,0:T(8,128)}) fusion(f32[128]{0:T(128)S(1)} %get-tuple-element.7, f32[128]{0:T(128)S(1)} %get-tuple-element.8, f32[1088]{0:T(1024)S(1)} %add_convert_fusion), kind=kLoop, calls=%fused_computation.2 | loop fusion | flops 278528 | bytes 1119488 | tf_op jit(solution)/shard_map/mul | solution.py:397
  4.2 121.9 %prefill_decode.1 = bf16[64,512]{1,0:T(8,128)(2,1)} custom-call(bf16[512,8192]{1,0:T(8,128)(2,1)} %refs_0_.1, bf16[64,8192]{1,0:T(8,128)(2,1)} %bitcast.4, bf16[512,512]{1,0:T(8,128)(2,1)} %refs_2_.1, bf16[512,512]{1,0:T(8,128)(2,1)} %refs_3_.1, bf16[8192,256]{1,0:T(8,128)(2,1)} %refs_4_.1, bf16[256,8192]{1,0:T(8,128)(2,1)} %refs_5_.1, ...), custom_call_target="tpu_custom_call" | custom-call | tf_op jit(solution)/shard_map/prefill_decode/pallas_call | solution.py:427
  126.0 1.5 %copy.9 = bf16[2,32,512]{2,1,0:T(8,128)(2,1)} copy(bf16[2,32,512]{2,1,0:T(8,128)(2,1)} %bitcast.5) | data formatting | bytes 131072
  (5 shorter events, 0.0 us)

commit v2 on v1

--- a/solution.py
+++ b/solution.py
@@ -2,6 +2,7 @@
 
 import jax
 import jax.numpy as jnp
+import numpy as np
 from jax import lax
 from jax.experimental import pallas as pl
 from jax.experimental.pallas import tpu as pltpu
@@ -15,6 +16,7 @@
 HALF = KV_HEADS // 2 * HEAD_DIM
 LOW = -1e30
 TAIL = 16
+CHUNKS = 2
 MESH = pl.DeviceIdType.MESH
 ROPE_BASE = 1000000.0
 
@@ -34,17 +36,18 @@
 
 def kernel(cfg, *refs):
     groups, devices, near, samples, heads, masked = cfg
-    (states, step, wk, wv, wq, wo, cosine, sine) = refs[:8]
+    (states, step, wk, wv, wq, wo, page_table, frequency) = refs[:8]
     refs = refs[8:]
     if masked:
         token_prompt, query_prompt = refs[:2]
         refs = refs[2:]
-    (out, st, wbuf, wqb, wob, acc, kb, vb, qown, qbuf, pout, pbuf, nk, nkr, tbuf, prbuf, sbuf, rbuf,
+    (out, cosine, sine, st, wbuf, wqb, wob, acc, kb, vb, qown, qbuf, pout, pbuf, nk, nkr, tbuf, prbuf, sbuf, rbuf,
      load_sem, send_sem, wsem, st_sem, qsem, psem, nsem, pair_sem, rsem) = refs
     chips = devices // 2
     deep = chips // near
     rows = wk.shape[0]
     part = 2 * rows // groups
+    piece = part // CHUNKS
     own_parts = groups // 2
     tokens_here = states.shape[0]
     tokens = 2 * tokens_here
@@ -109,11 +112,14 @@
             pl.when(when)(copy.start)
         sends.append((copy, when))
 
+    def block_of(chip, which, chunk):
+        return (chip * groups + which) * CHUNKS + chunk
+
     def w_rows(block):
-        return pl.ds(aligned(block * part, part), part)
+        return pl.ds(aligned(block * piece, piece), piece)
 
     def send_own(src_row, block, core, target, when=None):
-        src_rows = pl.ds(src_row, part)
+        src_rows = pl.ds(src_row, piece)
         src_cols = pl.ds(aligned(core * HALF, HALF), HALF)
         send(wk.at[src_rows, src_cols], wbuf.at[w_rows(block), pl.ds(0, HALF)],
              wsem.at[block], target, when)
@@ -124,20 +130,36 @@
         view = wbuf.at[w_rows(block)]
         pltpu.make_async_copy(view, view, wsem.at[block]).wait()
 
-    owner = lax.div(g, own_parts)
-    line_row = aligned(lax.rem(g, own_parts) * part, part)
-    line_block = p * groups + g
-    for k in range(1, deep):
-        chip = flip(z, k) * near + y
-        for core in range(2):
-            send_own(line_row, line_block, core, (g, chip * 2 + core), c == owner)
+    def along(shift):
+        return lax.rem(z + shift + deep, deep)
+
+    def inside(shift):
+        return jnp.logical_and(z + shift >= 0, z + shift < deep)
+
+    def to_line(h, when):
+        which = c * own_parts + h
+        for chunk in range(CHUNKS):
+            for shift in (1, -1):
+                go = jnp.logical_and(when(which), inside(shift))
+                for core in range(2):
+                    target = (g, (along(shift) * near + y) * 2 + core)
+                    send_own(h * part + chunk * piece, block_of(p, which, chunk), core, target, go)
+
+    def to_near(chunk):
+        for h in range(own_parts):
+            for k in range(1, near):
+                chip = z * near + flip(y, k)
+                for core in range(2):
+                    send_own(h * part + chunk * piece, block_of(p, c * own_parts + h, chunk), core,
+                             (g, chip * 2 + core))
+
     for h in range(own_parts):
-        block = p * groups + c * own_parts + h
-        for k in range(1, near):
-            chip = z * near + flip(y, k)
-            for core in range(2):
-                send_own(h * part, block, core, (g, chip * 2 + core))
-        send_own(h * part, block, 1 - c, (g, mate))
+        to_line(h, lambda which: which == g)
+    to_near(0)
+    for h in range(own_parts):
+        for chunk in range(CHUNKS):
+            send_own(h * part + chunk * piece, block_of(p, c * own_parts + h, chunk), 1 - c,
+                     (g, mate))
     send(states, st.at[my_rows], st_sem, (g, mate))
 
     loads[0].wait()
@@ -153,6 +175,13 @@
     queries = lax.fori_loop(
         0, dim // depth, q_step, jnp.zeros((wide, heads * HEAD_DIM), jnp.float32)
     )
+    lane_row = lax.broadcasted_iota(jnp.int32, (1, HEAD_DIM), 1)
+    sign = jnp.where(lane_row < HEAD_DIM // 2, -1.0, 1.0)
+    rate = frequency[...]
+    late_row = lax.broadcasted_iota(jnp.int32, (wide, HEAD_DIM), 0) >= samples
+    step_angle = (PROMPT_PAGES * PAGE + jnp.where(late_row, 1.0, 0.0)) * rate
+    cosine[pl.ds(tokens, wide), :] = jnp.cos(step_angle)
+    sine[pl.ds(tokens, wide), :] = jnp.sin(step_angle) * sign
     step_cos = cosine[pl.ds(tokens, wide), :]
     step_sin = sine[pl.ds(tokens, wide), :]
     for h in range(heads):
@@ -170,28 +199,61 @@
     for k in range(chips):
         give(qown, qbuf.at[q_slot], qsem.at[q_slot], flip(p, k) * 2 + kv_core)
 
-    def cross(block):
+    def cross(block, when):
         view = wbuf.at[w_rows(block)]
         for k in range(1, groups):
-            send(view, view, wsem.at[block], (lax.rem(g + k, groups), me))
-
-    def second(k):
+            send(view, view, wsem.at[block], (lax.rem(g + k, groups), me), when)
+
+    def line(d):
+        for chunk in range(CHUNKS):
+            for shift in (d, -d):
+                here = inside(shift)
+                block = block_of(along(shift) * near + y, g, chunk)
+                pl.when(here)(functools.partial(w_wait, block))
+                view = wbuf.at[w_rows(block)]
+                on = -1 if shift > 0 else 1
+                for j in range(1, near):
+                    send(view, view, wsem.at[block], (g, (z * near + flip(y, j)) * 2 + c), here)
+                if d < deep - 1:
+                    send(view, view, wsem.at[block], (g, (along(on) * near + y) * 2 + c),
+                         jnp.logical_and(here, inside(on)))
+                if d > 1:
+                    cross(block, here)
+
+    def second(d):
         for j in range(1, near):
-            block = (flip(z, k) * near + flip(y, j)) * groups + g
-            w_wait(block)
-            cross(block)
-
-    for k in range(1, deep):
-        block = (flip(z, k) * near + y) * groups + g
-        w_wait(block)
-        view = wbuf.at[w_rows(block)]
-        for j in range(1, near):
-            send(view, view, wsem.at[block],
-                 (g, (z * near + flip(y, j)) * 2 + c))
-        cross(block)
-        if k > 1:
-            second(k - 1)
+            for chunk in range(CHUNKS):
+                for shift in (d, -d):
+                    here = inside(shift)
+                    block = block_of(along(shift) * near + flip(y, j), g, chunk)
+                    pl.when(here)(functools.partial(w_wait, block))
+                    cross(block, here)
+
+    line(1)
+    for h in range(own_parts):
+        to_line(h, lambda which: which != g)
+    for chunk in range(1, CHUNKS):
+        to_near(chunk)
+    for d in range(2, deep):
+        line(d)
+        second(d - 1)
     second(deep - 1)
+
+    page_row = lax.broadcasted_iota(jnp.int32, (tokens // PAGE, page_table.shape[1]), 0)
+    entry = lax.broadcasted_iota(jnp.int32, (tokens // PAGE, page_table.shape[1]), 1)
+    match = page_table[...] == page_row + p * (tokens // PAGE)
+    slot = jnp.sum(
+        jnp.where(match, lax.rem(entry, PROMPT_PAGES).astype(jnp.float32), 0.0),
+        axis=1, keepdims=True,
+    )
+    base_angle = slot * float(PAGE) * rate
+    base_cos, base_sin = jnp.cos(base_angle), jnp.sin(base_angle)
+    row_angle = lax.broadcasted_iota(jnp.int32, (PAGE, HEAD_DIM), 0).astype(jnp.float32) * rate
+    row_cos, row_sin = jnp.cos(row_angle), jnp.sin(row_angle)
+    for i in range(tokens // PAGE):
+        one_cos, one_sin = base_cos[i : i + 1], base_sin[i : i + 1]
+        cosine[pl.ds(i * PAGE, PAGE), :] = one_cos * row_cos - one_sin * row_sin
+        sine[pl.ds(i * PAGE, PAGE), :] = (one_sin * row_cos + one_cos * row_sin) * sign
 
     total_rows = tokens + wide
     tiles = 4
@@ -215,18 +277,21 @@
     other_rows = st.at[pl.ds(aligned((1 - c) * tokens_here, tokens_here), tokens_here)]
     pltpu.make_async_copy(other_rows, other_rows, st_sem).wait()
     for h in range(own_parts):
-        w_wait(p * groups + (1 - c) * own_parts + h)
+        for chunk in range(CHUNKS):
+            w_wait(block_of(p, (1 - c) * own_parts + h, chunk))
     multiply(p, True)
     for j in range(1, near):
         chip = z * near + flip(y, j)
         for h in range(groups):
-            w_wait(chip * groups + h)
+            for chunk in range(CHUNKS):
+                w_wait(block_of(chip, h, chunk))
         multiply(chip, False)
-    for k in range(1, deep):
-        for j in range(near):
+    for j in range(near):
+        for k in range(1, deep):
             chip = flip(z, k) * near + flip(y, j)
             for h in range(1, groups):
-                w_wait(chip * groups + lax.rem(g + h, groups))
+                for chunk in range(CHUNKS):
+                    w_wait(block_of(chip, lax.rem(g + h, groups), chunk))
             multiply(chip, False)
 
     for j in range(2):
@@ -377,30 +442,18 @@
     half = devices // 2
     lanes = heads * wide
 
-    page_ids = own_chip * chip_pages + jnp.arange(chip_pages, dtype=jnp.int32)
-    slots = jnp.sum(
-        jnp.where(
-            page_table[None, :] == page_ids[:, None],
-            jnp.arange(total_pages, dtype=jnp.int32)[None, :],
-            0,
-        ),
-        axis=1,
-    )
-    place = (slots % PROMPT_PAGES * PAGE)[:, None] + jnp.arange(PAGE, dtype=jnp.int32)[None, :]
-    later = PROMPT_PAGES * PAGE + jnp.repeat(jnp.arange(2, dtype=jnp.int32), samples)
-    position = jnp.concatenate([place.reshape(tokens), later]).astype(jnp.float32)
-    lane = jnp.arange(HEAD_DIM, dtype=jnp.int32)
-    order = (lane % (HEAD_DIM // 2)).astype(jnp.float32)
-    frequency = ROPE_BASE ** (-order * 2.0 / HEAD_DIM)
-    angle = position[:, None] * frequency[None, :]
-    cosine = jnp.cos(angle)
-    sine = jnp.where(lane < HEAD_DIM // 2, -1.0, 1.0)[None, :] * jnp.sin(angle)
-
+    order = np.arange(HEAD_DIM) % (HEAD_DIM // 2)
+    frequency = jnp.asarray((ROPE_BASE ** (-order * 2.0 / HEAD_DIM)).astype(np.float32))[None, :]
     deep = chips // near
+    own_parts = groups // 2
     send_count = (
-        4 * (deep - 1)
-        + groups // 2 * (4 * (near - 1) + 2)
-        + (deep - 1) * (near - 1 + near * (groups - 1))
+        CHUNKS * own_parts * (16 + 2 + 4 * (near - 1))
+        + 2 * CHUNKS * (deep - 1) * near
+        + 2 * CHUNKS * (deep - 2) * groups
+        - 2 * CHUNKS * (deep - 2) * 1
+        + 2 * CHUNKS * (deep - 1) * (near - 1) * (groups - 1)
+        - 2 * CHUNKS * (deep - 1)
+        + 2 * CHUNKS * (deep - 2)
         + 3 * chips
         + half
         + 1
@@ -413,11 +466,20 @@
         value_weight,
         query_weight,
         out_weight,
-        cosine,
-        sine,
+        page_table[None, :],
+        frequency,
     ]
     specs = [pl.BlockSpec(memory_space=pl.ANY)] * 6 + [pl.BlockSpec(memory_space=pltpu.VMEM)] * 2
     if masked:
+        page_ids = own_chip * chip_pages + jnp.arange(chip_pages, dtype=jnp.int32)
+        slots = jnp.sum(
+            jnp.where(
+                page_table[None, :] == page_ids[:, None],
+                jnp.arange(total_pages, dtype=jnp.int32)[None, :],
+                0,
+            ),
+            axis=1,
+        )
         token_prompt = jnp.repeat(slots // PROMPT_PAGES, PAGE)[:, None]
         query_prompt = jnp.tile(sample_order // (samples // prompts), 2 * heads)[None, :]
         args += [token_prompt, query_prompt]
@@ -430,6 +492,8 @@
         in_specs=specs,
         out_specs=pl.BlockSpec(memory_space=pltpu.VMEM),
         scratch_shapes=[
+            pltpu.VMEM((tokens + wide, HEAD_DIM), f32),
+            pltpu.VMEM((tokens + wide, HEAD_DIM), f32),
             pltpu.VMEM((tokens + wide, dim), bf16),
             pltpu.VMEM((dim, 2 * HALF), bf16),
             pltpu.VMEM((dim, heads * HEAD_DIM), bf16),
@@ -449,7 +513,7 @@
             pltpu.VMEM((chips, wide, cols), bf16),
             dma((6,)),
             dma((send_count,)),
-            dma((chips * groups,)),
+            dma((chips * groups * CHUNKS,)),
             dma,
             dma((half,)),
             dma((chips,)),

time: 128 us -> 113 us (0.88)
  Pallas kernels: 122 us -> 111 us
  other arithmetic: 4.09 us -> 0 us
    pallas_call x1, Pallas kernels: 122 us -> 111 us  [on_device(): pl.pallas_call(functools.partial(kernel, (groups, devices, near, samples,...]
    mul x2 -> x0, other arithmetic: 3.16 us -> none  [the longest x1 3.15 us: on_device(): sine = jnp.where(lane < HEAD_DIM // 2, -1.0, 1.0)[None, :] * jnp.sin(angle)]
where the time goes in v2:
time: 113 us; the launch traced here: 112 us
  Pallas kernels  111 us (98%)
  local copies, waits for them, and re-layouts  1.47 us (1%)
    pallas_call x1, Pallas kernels, on_device(): pl.pallas_call(functools.partial(kernel, (groups, devices, near, samples,...  111 us

profile of v2, /device:TPU:0, one launch (start us, length us, event | category | flops | bytes accessed | tf_op | source)
XLA Modules:
  0.0 112.4 jit_solution(7588192468904314140)
XLA Ops:
  0.0 111.0 %prefill_decode.1 = bf16[64,512]{1,0:T(8,128)(2,1)} custom-call(bf16[512,8192]{1,0:T(8,128)(2,1)} %refs_0_.1, bf16[64,8192]{1,0:T(8,128)(2,1)} %bitcast.3, bf16[512,512]{1,0:T(8,128)(2,1)} %refs_2_.1, bf16[512,512]{1,0:T(8,128)(2,1)} %refs_3_.1, bf16[8192,256]{1,0:T(8,128)(2,1)} %refs_4_.1, bf16[256,8192]{1,0:T(8,128)(2,1)} %refs_5_.1, s32[1,64]{1,0:T(1,128)} %bitcast.5, ...), custom_call_target="tpu_custom_call" | custom-call | tf_op jit(solution)/shard_map/prefill_decode/pallas_call | solution.py:489
  111.0 1.5 %copy.10 = bf16[2,32,512]{2,1,0:T(8,128)(2,1)} copy(bf16[2,32,512]{2,1,0:T(8,128)(2,1)} %bitcast.4) | data formatting | bytes 131072

commit v3 on v2

--- a/solution.py
+++ b/solution.py
@@ -85,9 +85,6 @@
     loads.append(
         pltpu.make_async_copy(wv.at[:, own_cols], wbuf.at[own_w, pl.ds(HALF, HALF)], load_sem.at[5])
     )
-    for load in loads:
-        load.start()
-
     barrier = pltpu.get_barrier_semaphore()
     for k in range(1, devices):
         pl.semaphore_signal(
@@ -161,43 +158,8 @@
             send_own(h * part + chunk * piece, block_of(p, c * own_parts + h, chunk), 1 - c,
                      (g, mate))
     send(states, st.at[my_rows], st_sem, (g, mate))
-
-    loads[0].wait()
-    loads[1].wait()
-    depth = 1024
-
-    def q_step(i, total):
-        at = pl.ds(aligned(i * depth, depth), depth)
-        return total + jnp.dot(
-            st[pl.ds(tokens, wide), at], wqb[at, :], preferred_element_type=jnp.float32
-        )
-
-    queries = lax.fori_loop(
-        0, dim // depth, q_step, jnp.zeros((wide, heads * HEAD_DIM), jnp.float32)
-    )
-    lane_row = lax.broadcasted_iota(jnp.int32, (1, HEAD_DIM), 1)
-    sign = jnp.where(lane_row < HEAD_DIM // 2, -1.0, 1.0)
-    rate = frequency[...]
-    late_row = lax.broadcasted_iota(jnp.int32, (wide, HEAD_DIM), 0) >= samples
-    step_angle = (PROMPT_PAGES * PAGE + jnp.where(late_row, 1.0, 0.0)) * rate
-    cosine[pl.ds(tokens, wide), :] = jnp.cos(step_angle)
-    sine[pl.ds(tokens, wide), :] = jnp.sin(step_angle) * sign
-    step_cos = cosine[pl.ds(tokens, wide), :]
-    step_sin = sine[pl.ds(tokens, wide), :]
-    for h in range(heads):
-        one = queries[:, h * HEAD_DIM : (h + 1) * HEAD_DIM]
-        qown[pl.ds(h * wide, wide), :] = turn(one, step_cos, step_sin).astype(jnp.bfloat16)
-
-    def give(src, dst, sem, target):
-        send(src, dst, sem, (g, target), target != me)
-
-        @pl.when(target == me)
-        def _():
-            pltpu.make_async_copy(src, dst, sem).start()
-
-    q_slot = lax.rem(me, half)
-    for k in range(chips):
-        give(qown, qbuf.at[q_slot], qsem.at[q_slot], flip(p, k) * 2 + kv_core)
+    for load in loads:
+        load.start()
 
     def cross(block, when):
         view = wbuf.at[w_rows(block)]
@@ -238,6 +200,43 @@
         line(d)
         second(d - 1)
     second(deep - 1)
+
+    loads[0].wait()
+    loads[1].wait()
+    depth = 1024
+
+    def q_step(i, total):
+        at = pl.ds(aligned(i * depth, depth), depth)
+        return total + jnp.dot(
+            st[pl.ds(tokens, wide), at], wqb[at, :], preferred_element_type=jnp.float32
+        )
+
+    queries = lax.fori_loop(
+        0, dim // depth, q_step, jnp.zeros((wide, heads * HEAD_DIM), jnp.float32)
+    )
+    lane_row = lax.broadcasted_iota(jnp.int32, (1, HEAD_DIM), 1)
+    sign = jnp.where(lane_row < HEAD_DIM // 2, -1.0, 1.0)
+    rate = frequency[...]
+    late_row = lax.broadcasted_iota(jnp.int32, (wide, HEAD_DIM), 0) >= samples
+    step_angle = (PROMPT_PAGES * PAGE + jnp.where(late_row, 1.0, 0.0)) * rate
+    cosine[pl.ds(tokens, wide), :] = jnp.cos(step_angle)
+    sine[pl.ds(tokens, wide), :] = jnp.sin(step_angle) * sign
+    step_cos = cosine[pl.ds(tokens, wide), :]
+    step_sin = sine[pl.ds(tokens, wide), :]
+    for h in range(heads):
+        one = queries[:, h * HEAD_DIM : (h + 1) * HEAD_DIM]
+        qown[pl.ds(h * wide, wide), :] = turn(one, step_cos, step_sin).astype(jnp.bfloat16)
+
+    def give(src, dst, sem, target):
+        send(src, dst, sem, (g, target), target != me)
+
+        @pl.when(target == me)
+        def _():
+            pltpu.make_async_copy(src, dst, sem).start()
+
+    q_slot = lax.rem(me, half)
+    for k in range(chips):
+        give(qown, qbuf.at[q_slot], qsem.at[q_slot], flip(p, k) * 2 + kv_core)
 
     page_row = lax.broadcasted_iota(jnp.int32, (tokens // PAGE, page_table.shape[1]), 0)
     entry = lax.broadcasted_iota(jnp.int32, (tokens // PAGE, page_table.shape[1]), 1)

time: 113 us -> 109 us (0.965)
  Pallas kernels: 111 us -> 108 us
    pallas_call x1, Pallas kernels: 111 us -> 108 us  [on_device(): pl.pallas_call(functools.partial(kernel, (groups, devices, near, samples,...]
where the time goes in v3:
time: 109 us
  Pallas kernels  108 us (99%)
  local copies, waits for them, and re-layouts  1.47 us (1%)
    pallas_call x1, Pallas kernels, on_device(): pl.pallas_call(functools.partial(kernel, (groups, devices, near, samples,...  108 us

profile of v3, /device:TPU:0, one launch (start us, length us, event | category | flops | bytes accessed | tf_op | source)
XLA Modules:
  0.0 109.2 jit_solution(1574578238936722013)
XLA Ops:
  0.0 107.7 %prefill_decode.1 = bf16[64,512]{1,0:T(8,128)(2,1)} custom-call(bf16[512,8192]{1,0:T(8,128)(2,1)} %refs_0_.1, bf16[64,8192]{1,0:T(8,128)(2,1)} %bitcast.3, bf16[512,512]{1,0:T(8,128)(2,1)} %refs_2_.1, bf16[512,512]{1,0:T(8,128)(2,1)} %refs_3_.1, bf16[8192,256]{1,0:T(8,128)(2,1)} %refs_4_.1, bf16[256,8192]{1,0:T(8,128)(2,1)} %refs_5_.1, s32[1,64]{1,0:T(1,128)} %bitcast.5, ...), custom_call_target="tpu_custom_call" | custom-call | tf_op jit(solution)/shard_map/prefill_decode/pallas_call | solution.py:488
  107.7 1.5 %copy.10 = bf16[2,32,512]{2,1,0:T(8,128)(2,1)} copy(bf16[2,32,512]{2,1,0:T(8,128)(2,1)} %bitcast.4) | data formatting | bytes 131072
